TPU v7x, 32 devices: a whole 2x2x4 slice. The times are simulated.
32 devices in a mesh: row: 8 (over z, y), col: 4 (over x, core).
Axes of the slice: x: 2, y: 2, z: 4, core: 2. Of those that a mesh axis runs over, the one named last changes fastest.
Arguments:
- query_acts: bfloat16 [256, 8192], P('col', 'row'), may hold values from -6 to 6
- query_grads: bfloat16 [256, 28672], P('row', 'col'), may hold values from -6 to 6
- ritz_mats: float32 [3, 8192, 28672], P(None, 'row', 'col'), may hold values from -0.095683193 to 0.095683193, as said below
- eigenvalues: float32 [3], replicated, may hold values from 0.5 to 4
- train_acts: bfloat16 [64, 8192], P('row'), may hold values from -6 to 6
- train_grads: bfloat16 [64, 28672], P('row', 'col'), may hold values from -6 to 6
Outputs:
- response: bfloat16 [64, 28672], P('row', 'col')
- scores: float32 [64], P('row')
Inputs may be any that keep to these rules, and one draw needn't show every extreme that they name: `ritz_mats`: real entries of order one over the square root of 8192; every matrix has full rank.
All inputs are finite; a program needn't handle non-finite values.
Results may differ from a plain program's by a relative error of at most 0.0012.
Values may be sent and summed in bfloat16 or wider, within the bound.
No kernel may reach another device: no remote copies, remote signals or barrier semaphores. Data moves between devices by JAX's collectives and lax.ppermute only.
A program may use at most 192 MiB of HBM per device.

v0:
```python
import math

import jax
import jax.numpy as jnp
from jax import lax
from jax.sharding import PartitionSpec as P

D_OUT = 28672
QUERY = 256


highest = lax.Precision.HIGHEST


def per_device(query_acts, query_grads, ritz_mats, eigenvalues, train_acts, train_grads):
    outer_cols = ritz_mats.shape[2]
    acts_all = lax.all_gather(query_acts, "col", axis=0, tiled=True)
    grad_tile = lax.dot_general(
        acts_all,
        lax.all_gather(query_grads, "row", axis=0, tiled=True),
        (((0,), (0,)), ((), ())),
        preferred_element_type=jnp.float32,
    )
    local_terms = jnp.sum(ritz_mats * grad_tile[None], axis=(1, 2))
    coeffs = lax.psum(local_terms, ("row", "col"))
    weights = coeffs / (eigenvalues * math.sqrt(QUERY * D_OUT))
    train_local = lax.all_to_all(train_acts, "row", split_axis=1, concat_axis=0, tiled=True).astype(
        jnp.float32
    )
    root_width = math.sqrt(D_OUT)
    total = jnp.zeros((lax.axis_size("row") * train_acts.shape[0], outer_cols), jnp.float32)
    for which in range(ritz_mats.shape[0]):
        total = total + weights[which] * jnp.dot(train_local, ritz_mats[which], precision=highest)
    response_full = lax.psum_scatter(total, "row", scatter_dimension=0, tiled=True)
    score_terms = jnp.sum(response_full * train_grads.astype(jnp.float32), axis=1) / root_width
    scores = lax.psum(score_terms, "col")
    response = response_full.astype(jnp.bfloat16)
    return (response, scores)


def solution(mesh):
    in_specs = (
        P("col", "row"),
        P("row", "col"),
        P(None, "row", "col"),
        P(),
        P("row", None),
        P("row", "col"),
    )
    out_specs = (P("row", "col"), P("row"))
    return jax.shard_map(
        per_device, mesh=mesh, in_specs=in_specs, out_specs=out_specs, check_vma=False
    )
```

profile of v0, /device:TPU:0, one launch (start us, length us, event | category | flops | bytes accessed | tf_op | source)
XLA Modules:
  0.0 306.3 jit_solution(11983988093099938950)
XLA Ops:
  7.2 0.0 all-gather.2.cloned.1.call-start
  7.2 0.7 all-gather.2.cloned.1.call-update
  7.9 8.9 %all_gather.6 = bf16[256,1024]{1,0:T(8,128)(2,1)S(1)} all-gather(bf16[64,1024]{1,0:T(8,128)(2,1)} %param.6), channel_id=1, replica_groups=mesh['row'=8,'col'=4] {'col'}, dimensions={0}, use_global_device_ids=true | all-gather | bytes 655360 | tf_op jit(solution)/shard_map/all_gather | solution.py:17
  16.8 62.4 %all-gather.2.cloned.1.call-done = bf16[256,7168]{1,0:T(8,128)(2,1)} async-done(((bf16[32,7168]{1,0:T(8,128)(2,1)}), bf16[256,7168]{1,0:T(8,128)(2,1)}) %all-gather.2.cloned.1.call-update) | async-done | bytes 3670032 | tf_op jit(solution)/shard_map/all_gather | solution.py:20
  79.1 13.7 %fusion.28 = f32[1024,7168]{1,0:T(8,128)} fusion(bf16[256,1024]{1,0:T(8,128)(2,1)S(1)} %all_gather.6, bf16[256,7168]{1,0:T(8,128)(2,1)} %all-gather.2.cloned.1.call-done), kind=kOutput, calls=%fused_computation.22 | convolution fusion | flops 3758096384 | bytes 33554432 | tf_op jit(solution)/shard_map/dot_general | solution.py:18
  92.8 0.0 copy-start.1
  92.8 35.5 %multiply_reduce_fusion = f32[3]{0:T(128)S(1)} fusion(f32[3,1024,7168]{2,1,0:T(8,128)} %param.8, f32[1024,7168]{1,0:T(8,128)} %fusion.28), kind=kLoop, calls=%fused_computation | loop fusion | flops 44040188 | bytes 117440528 | tf_op jit(solution)/shard_map/reduce_sum | solution.py:24
  128.4 3.4 %all-to-all-start = ((bf16[8,8,1024]{2,0,1:T(8,128)(2,1)}), bf16[8,8,1024]{2,0,1:T(8,128)(2,1)S(1)}, u32[]{:S(2)}, u32[]{:S(2)}) async-start(bf16[8,8,1024]{2,0,1:T(8,128)(2,1)} %bitcast.1), calls=%async_computation | async-start | bytes 262144 | tf_op jit(solution)/shard_map/all_to_all | solution.py:27
  131.8 0.0 reduce-scatter.2.cloned.1.call-start
  131.8 40.7 %psum.14 = f32[3]{0:T(128)S(1)} all-reduce(f32[3]{0:T(128)S(1)} %multiply_reduce_fusion), channel_id=1, replica_groups=mesh['row'=8,'col'=4] {'row','col'}, use_global_device_ids=true, to_apply=%region_1.0 | all-reduce | flops 3 | bytes 24 | tf_op jit(solution)/shard_map/psum | solution.py:25
  172.5 0.0 copy-done.1
  172.5 0.7 fusion.27
  173.2 0.0 all-to-all-done
  173.2 15.6 %fusion.15 = f32[64,7168]{1,0:T(8,128)S(1)} fusion(f32[3,1024,7168]{2,1,0:T(8,128)} %param.8, f32[]{:T(128)} %bitcast.5, bf16[8,8,1024]{2,0,1:T(8,128)(2,1)S(1)} %all-to-all-done), kind=kOutput, calls=%fused_computation.12 | convolution fusion | flops 5637603328 | bytes 31326720 | tf_op jit(solution)/shard_map/dot_general | solution.py:33
  188.8 18.0 %fusion.12 = f32[64,7168]{1,0:T(8,128)S(1)} fusion(f32[64,7168]{1,0:T(8,128)S(1)} %fusion.15, f32[3,1024,7168]{2,1,0:T(8,128)} %param.8, f32[]{:T(128)} %bitcast, bf16[8,8,1024]{2,0,1:T(8,128)(2,1)S(1)} %all-to-all-done), kind=kOutput, calls=%fused_computation.11 | convolution fusion | flops 5638062080 | bytes 33161728 | tf_op jit(solution)/shard_map/dot_general | solution.py:33
  206.8 0.0 copy-start
  206.8 17.5 %fusion.21 = f32[64,7168]{1,0:T(8,128)} fusion(f32[64,7168]{1,0:T(8,128)S(1)} %fusion.12, f32[3,1024,7168]{2,1,0:T(8,128)} %param.8, f32[]{:T(128)} %bitcast.8, bf16[8,8,1024]{2,0,1:T(8,128)(2,1)S(1)} %all-to-all-done), kind=kOutput, calls=%fused_computation.14 | convolution fusion | flops 5638062080 | bytes 33161728 | tf_op jit(solution)/shard_map/dot_general | solution.py:33
  224.3 0.0 reduce-scatter.2.cloned.1.call-update
  224.3 67.2 %reduce-scatter.2.cloned.1.call-done = f32[8,7168]{1,0:T(8,128)} async-done(((f32[64,7168]{1,0:T(8,128)}), f32[8,7168]{1,0:T(8,128)}) %reduce-scatter.2.cloned.1.call-update) | async-done | bytes 229392 | tf_op jit(solution)/shard_map/reduce_scatter | solution.py:34
  291.5 0.0 copy-done
  291.5 1.8 multiply_reduce_fusion.1
  293.3 6.2 %psum.15 = f32[8]{0:T(128)} all-reduce(f32[8]{0:T(128)S(1)} %broadcast_multiply_fusion), channel_id=1, replica_groups=mesh['row'=8,'col'=4] {'col'}, use_global_device_ids=true, to_apply=%region_4.0 | all-reduce | flops 8 | bytes 64 | tf_op jit(solution)/shard_map/psum | solution.py:36
  (2 shorter events, 0.0 us)
Async XLA Ops:
  7.2 72.0 %all-gather.2.cloned.1.call-start = ((), (), s32[]{:S(2)}) async-start(), calls=%async_computation.2 | async-start | bytes 4128768 | tf_op jit(solution)/shard_map/all_gather | solution.py:20
  92.8 79.7 %copy-start.1 = (f32[3]{0:T(128)S(1)}, f32[3]{0:T(128)}, u32[]{:S(2)}) copy-start(f32[3]{0:T(128)} %param.9) | copy-start | bytes 40
  128.4 44.8 %all-to-all-start = ((bf16[8,8,1024]{2,0,1:T(8,128)(2,1)}), bf16[8,8,1024]{2,0,1:T(8,128)(2,1)S(1)}, u32[]{:S(2)}, u32[]{:S(2)}) async-start(bf16[8,8,1024]{2,0,1:T(8,128)(2,1)} %bitcast.1), calls=%async_computation | async-start | bytes 262144 | tf_op jit(solution)/shard_map/all_to_all | solution.py:27
  131.8 159.8 %reduce-scatter.2.cloned.1.call-start = ((), (), s32[]{:S(2)}) async-start(), calls=%async_computation.3 | async-start | bytes 2064384 | tf_op jit(solution)/shard_map/reduce_scatter | solution.py:34
  206.8 84.7 %copy-start = (bf16[8,7168]{1,0:T(8,128)(2,1)S(1)}, bf16[8,7168]{1,0:T(8,128)(2,1)}, u32[]{:S(2)}) copy-start(bf16[8,7168]{1,0:T(8,128)(2,1)} %param.11) | copy-start | bytes 344068
Sparse Core Ops, SparseCore 0:
  10.2 68.9 all-gather.1
  224.4 67.0 reduce-scatter.1
where the time goes:
time: 307 us; the launch traced here: 306 us
  waiting for transfers between devices  130 us (42%)
  matrix products  64.8 us (21%)
  blocking collectives  55.7 us (18%)
  other arithmetic  37.4 us (12%)
  between operations  14.1 us (5%)
  starting transfers between devices  3.46 us (1%)
    reduce_scatter x1, waiting for transfers between devices, per_device(): lax.psum_scatter(total, 'row', scatter_dimension=0, tiled=True)  67.2 us
    all_gather x1, waiting for transfers between devices, per_device(): lax.all_gather(query_grads, 'row', axis=0, tiled=True)  62.4 us
    dot_general x3, matrix products, per_device(): jnp.dot(train_local, ritz_mats[which], precision=highest)  51.1 us
    psum x1, blocking collectives, per_device(): coeffs = lax.psum(local_terms, ('row', 'col'))  40.7 us
    reduce_sum x1, other arithmetic, per_device(): local_terms = jnp.sum(ritz_mats * grad_tile[None], axis=(1, 2))  35.5 us
    dot_general x1, matrix products, per_device(): lax.dot_general(acts_all, lax.all_gather(query_grads, 'row', axis=0, tile...  13.7 us
    all_gather x1, blocking collectives, per_device(): acts_all = lax.all_gather(query_acts, 'col', axis=0, tiled=True)  8.86 us
    psum x1, blocking collectives, per_device(): scores = lax.psum(score_terms, 'col')  6.17 us
  transfers between devices with their start and end apart: 3, of which 2 were waited for; matrix products, arithmetic and copies ran while one was open for 0% of the time, Pallas kernels for 0%

commit v1 on v0

v1 whole, which is shorter than its diff:
```python
import functools
import math

import jax
import jax.numpy as jnp
from jax import lax
from jax.experimental import pallas as pl
from jax.experimental.pallas import tpu as pltpu
from jax.sharding import PartitionSpec as P


LANES = 128
TILE = 1024
ROWS = 512
SUB = 256
CHUNKS = (1, 2, 2, 2)
EARLY = 2


def pass_kernel(lines, n_pieces, x_ref, at_ref, *refs):
    g_refs = refs[:n_pieces]
    r_ref, keep_ref, send_ref, c_ref, g_buf, t_buf = refs[n_pieces:]
    n_ritz, rows, width = r_ref.shape
    tokens = x_ref.shape[0]
    block = pl.program_id(1)

    me = lax.axis_index("row")
    z, y = me // 2, me % 2
    slots = [(z ^ m) * 2 + side for side in (y, 1 - y) for m in range(lines)]
    col = lax.axis_index("col")
    homes = [(z ^ m ^ col) * 2 + side for side in (y, 1 - y) for m in range(lines)]

    @pl.when((pl.program_id(0) == 0) & (block == 0))
    def _():
        c_ref[...] = jnp.zeros_like(c_ref)

    @pl.when(block == 0)
    def _():
        t_buf[...] = jnp.zeros_like(t_buf)
        if not lines:
            g_buf[...] = g_refs[0][...]
        else:
            share = g_buf.shape[0] // len(homes)
            todo = iter(homes)
            for ref in g_refs:
                for at in range(0, ref.shape[0], share):
                    start = pl.multiple_of(next(todo) * share, share)
                    g_buf[pl.ds(start, share), :] = ref[at : at + share, :]

    first = pl.multiple_of(block * rows, rows)
    a = at_ref[pl.ds(first, rows), :]
    x = x_ref[:, pl.ds(first, rows)]
    for lane in range(0, width, SUB):
        cols = slice(lane, lane + SUB)
        q = jnp.dot(a, g_buf[:, cols], preferred_element_type=jnp.float32)
        for k in range(n_ritz):
            r = r_ref[k, :, cols]
            part = jnp.sum((r * q).reshape(rows // 8, 8, SUB), axis=0)
            for at in range(0, SUB, LANES):
                c_ref[k] += part[:, at : at + LANES]
            high = r.astype(jnp.bfloat16)
            low = (r - high.astype(jnp.float32)).astype(jnp.bfloat16)
            t_buf[k, :, cols] += jnp.dot(x, high, preferred_element_type=jnp.float32) + jnp.dot(
                x, low, preferred_element_type=jnp.float32
            )

    @pl.when(block == pl.num_programs(1) - 1)
    def _():
        if not lines:
            keep_ref[...] = t_buf[:, : tokens // 2, :]
            send_ref[...] = t_buf[:, tokens // 2 :, :]
        else:
            share = tokens // len(slots)
            for n, slot in enumerate(slots):
                ref = keep_ref if n < lines else send_ref
                at = n % lines * share
                start = pl.multiple_of(slot * share, share)
                ref[:, at : at + share, :] = t_buf[:, pl.ds(start, share), :]


def one_pass(lines, x, at, pieces, offsets, ritz, offset, width, tile):
    n_ritz, rows, _ = ritz.shape
    tokens = x.shape[0]
    depth = min(ROWS, rows)
    first = offset // tile
    queries = at.shape[1]

    def columns(start):
        return lambda j, i: (0, start // tile + j)

    specs = [
        pl.BlockSpec((piece.shape[0], tile), columns(start)) for piece, start in zip(pieces, offsets)
    ]
    half = pl.BlockSpec((n_ritz, tokens // 2, tile), lambda j, i: (0, 0, j))
    return pl.pallas_call(
        functools.partial(pass_kernel, lines, len(pieces)),
        grid=(width // tile, rows // depth),
        in_specs=[
            pl.BlockSpec((tokens, rows), lambda j, i: (0, 0)),
            pl.BlockSpec((rows, queries), lambda j, i: (0, 0)),
            *specs,
            pl.BlockSpec((n_ritz, depth, tile), lambda j, i: (0, i, first + j)),
        ],
        out_specs=[
            half,
            half,
            pl.BlockSpec((n_ritz, 8, LANES), lambda j, i: (0, 0, 0)),
        ],
        out_shape=[
            jax.ShapeDtypeStruct((n_ritz, tokens // 2, width), jnp.float32),
            jax.ShapeDtypeStruct((n_ritz, tokens // 2, width), jnp.float32),
            jax.ShapeDtypeStruct((n_ritz, 8, LANES), jnp.float32),
        ],
        scratch_shapes=[
            pltpu.VMEM((queries, tile), jnp.bfloat16),
            pltpu.VMEM((n_ritz, tokens, tile), jnp.float32),
        ],
        compiler_params=pltpu.CompilerParams(
            dimension_semantics=("arbitrary", "arbitrary"), vmem_limit_bytes=28 * 2**20
        ),
        cost_estimate=pl.CostEstimate(
            flops=2 * rows * width * (queries + 2 * n_ritz * tokens),
            bytes_accessed=n_ritz * rows * width * 4,
            transcendentals=0,
        ),
        name="one_pass",
    )(x, at, *pieces, ritz)


def swap(value, mask, axis="row"):
    size = lax.axis_size(axis)
    return lax.ppermute(value, axis, [(i, i ^ mask) for i in range(size)])


def sum_everywhere(parts):
    size = lax.axis_size("row") * lax.axis_size("col")
    block = jnp.pad(parts, ((0, 8 - parts.shape[0]), (0, 0)))
    mine = jnp.broadcast_to(block[None], (size, *block.shape))
    theirs = lax.all_to_all(mine, ("row", "col"), 0, 0)
    return jnp.sum(theirs, axis=(0, 2))[: parts.shape[0]]


def blend(weights, terms):
    total = weights[0] * terms[0]
    for k in range(1, terms.shape[0]):
        total = total + weights[k] * terms[k]
    return total


def blend_kernel(n_terms, n_add, w_ref, *refs):
    terms, adds, outs = refs[:n_terms], refs[n_terms : n_terms + n_add], refs[n_terms + n_add :]
    total = None
    for k in range(terms[0].shape[0]):
        value = terms[0][k]
        for ref in terms[1:]:
            value = value + ref[k]
        total = w_ref[k] * value if total is None else total + w_ref[k] * value
    for ref in adds:
        total = total + ref[...]
    share = outs[0].shape[0]
    for n, ref in enumerate(outs):
        ref[...] = total[n * share : (n + 1) * share]


def blended(weights, terms, adds, pieces):
    n_ritz, tokens, width = terms[0].shape
    share = tokens // pieces
    tile = min(width, TILE)
    return pl.pallas_call(
        functools.partial(blend_kernel, len(terms), len(adds)),
        grid=(width // tile,),
        in_specs=[pl.BlockSpec(memory_space=pltpu.SMEM)]
        + [pl.BlockSpec((n_ritz, tokens, tile), lambda j: (0, 0, j))] * len(terms)
        + [pl.BlockSpec((tokens, tile), lambda j: (0, j))] * len(adds),
        out_specs=[pl.BlockSpec((share, tile), lambda j: (0, j))] * pieces,
        out_shape=[jax.ShapeDtypeStruct((share, width), jnp.float32)] * pieces,
        compiler_params=pltpu.CompilerParams(
            dimension_semantics=("arbitrary",), vmem_limit_bytes=8 * 2**20
        ),
        cost_estimate=pl.CostEstimate(
            flops=2 * len(terms) * terms[0].size,
            bytes_accessed=4 * len(terms) * terms[0].size,
            transcendentals=0,
        ),
        name="blended",
    )(weights, *terms, *adds)


def per_device(query_acts, query_grads, ritz_mats, eigenvalues, train_acts, train_grads, *, d_out):
    n_row, n_col = lax.axis_size("row"), lax.axis_size("col")
    width = ritz_mats.shape[2]
    scale = eigenvalues * math.sqrt(n_col * query_acts.shape[0] * d_out)
    root_width = math.sqrt(d_out)

    if not chunked(n_row, n_col):
        x = lax.all_to_all(train_acts, "row", split_axis=1, concat_axis=0, tiled=True)
        acts_all = lax.all_gather(query_acts, "col", axis=0, tiled=True)
        grads_all = lax.all_gather(query_grads, "row", axis=0, tiled=True)
        first, second, parts = one_pass(
            0, x, acts_all.T, [grads_all], [0], ritz_mats, 0, width, 512
        )
        coeffs = lax.psum(jnp.sum(parts, axis=(1, 2)), ("row", "col"))
        total = blend(coeffs / scale, jnp.concatenate([first, second], axis=1))
        response_full = lax.psum_scatter(total, "row", scatter_dimension=0, tiled=True)
        score_terms = jnp.sum(response_full * train_grads.astype(jnp.float32), axis=1)
        scores = lax.psum(score_terms / root_width, "col")
        return response_full.astype(jnp.bfloat16), scores

    lines = n_row // 2
    x = lax.all_to_all(train_acts, "row", split_axis=1, concat_axis=0, tiled=True)
    acts = [query_acts] + [swap(query_acts, m, "col") for m in range(1, n_col)]
    at = jnp.concatenate(acts, axis=0).T
    line, offsets = [], []
    offset = 0
    for n, tiles in enumerate(CHUNKS):
        piece = query_grads[:, offset : offset + tiles * TILE]
        line.append([swap(piece, 2 * m) for m in range(1, lines)])
        if n == 0:
            partner = swap(query_grads, 1)
        offsets.append(offset)
        offset += tiles * TILE

    keeps, sends, parts = [], [], []
    for n, tiles in enumerate(CHUNKS):
        across = swap(jnp.concatenate(line[n], axis=0), 1)
        keep, send, part = one_pass(
            lines,
            x,
            at,
            [query_grads, *line[n], partner, across],
            [offsets[n], 0, 0, 0, offsets[n], 0],
            ritz_mats,
            offsets[n],
            tiles * TILE,
            TILE,
        )
        if n < EARLY:
            send = swap(send, 1)
        keeps.append(keep)
        sends.append(send)
        parts.append(part)
    coeffs = sum_everywhere(jnp.sum(sum(parts), axis=1))
    weights = coeffs / scale

    theirs = {}
    for n in range(EARLY, len(CHUNKS)):
        theirs[n] = swap(blended(weights, [sends[n]], [], 1)[0], 1)
    responses, score_terms = [], 0.0
    for n, tiles in enumerate(CHUNKS):
        if n < EARLY:
            held = blended(weights, [keeps[n], sends[n]], [], lines)
        else:
            held = blended(weights, [keeps[n]], [theirs[n]], lines)
        total = held[0]
        for m in range(1, lines):
            total = total + swap(held[m], 2 * m)
        responses.append(total.astype(jnp.bfloat16))
        grads = train_grads[:, offsets[n] : offsets[n] + tiles * TILE].astype(jnp.float32)
        score_terms = score_terms + jnp.sum(total * grads, axis=1)
    scores = lax.psum(score_terms / root_width, "col")
    return jnp.concatenate(responses, axis=1), scores


def chunked(n_row, n_col):
    return n_row == 8 and n_col == 4


def solution(mesh):
    in_specs = (
        P("col", "row"),
        P("row", "col"),
        P(None, "row", "col"),
        P(),
        P("row", None),
        P("row", "col"),
    )
    out_specs = (P("row", "col"), P("row"))

    def program(query_acts, query_grads, ritz_mats, eigenvalues, train_acts, train_grads):
        body = functools.partial(per_device, d_out=ritz_mats.shape[2])
        return jax.shard_map(
            body, mesh=mesh, in_specs=in_specs, out_specs=out_specs, check_vma=False
        )(query_acts, query_grads, ritz_mats, eigenvalues, train_acts, train_grads)

    return program
```

time: 307 us -> 170 us (0.55)
  waiting for transfers between devices: 130 us -> 32.4 us
  matrix products: 64.8 us -> 0 us
  starting transfers between devices: 3.46 us -> 63.2 us
  blocking collectives: 55.7 us -> 6.17 us
  Pallas kernels: 0 us -> 45.6 us
  other arithmetic: 37.4 us -> 7.03 us
  local copies, waits for them, and re-layouts: 0.68 us -> 14.3 us
  between operations: 14.1 us -> 0.98 us
    reduce_scatter x1 -> x0, waiting for transfers between devices: 67.2 us -> none  [per_device(): lax.psum_scatter(total, 'row', scatter_dimension=0, tiled=True)]
    dot_general x4 -> x0, matrix products: 64.8 us -> none  [the longest x3 51.1 us: per_device(): jnp.dot(train_local, ritz_mats[which], precision=highest)]
    all_gather x1 -> x0, waiting for transfers between devices: 62.4 us -> none  [per_device(): lax.all_gather(query_grads, 'row', axis=0, tiled=True)]
    ppermute x0 -> x36, starting transfers between devices: none -> 51.7 us  [swap(): return lax.ppermute(value, axis, [(i, i ^ mask) for i in range(size)])]
    pallas_call x0 -> x10, Pallas kernels: none -> 45.6 us  [the longest x4 41.5 us: one_pass(): pl.pallas_call(functools.partial(pass_kernel, lines, len(pieces)), grid=(...]
    psum x2 -> x1, blocking collectives: 46.9 us -> 6.17 us  [per_device(): scores = lax.psum(score_terms / root_width, 'col')]
    reduce_sum x2 -> x4, other arithmetic: 37.3 us -> 1.99 us  [the longest x2 1.82 us: per_device(): score_terms = score_terms + jnp.sum(total * grads, axis=1)]
    ppermute x0 -> x36, waiting for transfers between devices: none -> 25.9 us  [swap(): return lax.ppermute(value, axis, [(i, i ^ mask) for i in range(size)])]
  transfers between devices with their start and end apart: 3 -> 38, of which waited for: 2 -> 13; matrix products, arithmetic and copies ran while one was open for 0% -> 5% of each run, Pallas kernels for 0% -> 27%
where the time goes in v1:
time: 170 us
  starting transfers between devices  63.2 us (37%)
  Pallas kernels  45.6 us (27%)
  waiting for transfers between devices  32.4 us (19%)
  local copies, waits for them, and re-layouts  14.3 us (8%)
  other arithmetic  7.03 us (4%)
  blocking collectives  6.17 us (4%)
    ppermute x36, starting transfers between devices, swap(): return lax.ppermute(value, axis, [(i, i ^ mask) for i in range(size)])  51.7 us
    pallas_call x4, Pallas kernels, one_pass(): pl.pallas_call(functools.partial(pass_kernel, lines, len(pieces)), grid=(...  41.5 us
    ppermute x36, waiting for transfers between devices, swap(): return lax.ppermute(value, axis, [(i, i ^ mask) for i in range(size)])  25.9 us
    unnamed x53, local copies, waits for them, and re-layouts  11.7 us
    all_to_all x1, waiting for transfers between devices, sum_everywhere(): theirs = lax.all_to_all(mine, ('row', 'col'), 0, 0)  6.47 us
    psum x1, blocking collectives, per_device(): scores = lax.psum(score_terms / root_width, 'col')  6.17 us
    all_to_all x1, starting transfers between devices, per_device(): lax.all_to_all(train_acts, 'row', split_axis=1, concat_axis=0, tiled=True)  5.98 us
    all_to_all x1, starting transfers between devices, sum_everywhere(): theirs = lax.all_to_all(mine, ('row', 'col'), 0, 0)  5.51 us
  transfers between devices with their start and end apart: 38, of which 13 were waited for; matrix products, arithmetic and copies ran while one was open for 5% of the time, Pallas kernels for 27%

profile of v1, /device:TPU:0, one launch (start us, length us, event | category | flops | bytes accessed | tf_op | source)
XLA Modules:
  0.0 169.6 jit_solution(12768284055787330886)
XLA Ops:
  1.5 3.1 %collective-permute-start.3 = (bf16[32,1024]{1,0:T(8,128)(2,1)S(1)}, bf16[32,1024]{1,0:T(8,128)(2,1)S(1)}, u32[]{:S(2)}, u32[]{:S(2)}) collective-permute-start(bf16[32,1024]{1,0:T(8,128)(2,1)S(1)} %slice.27), channel_id=1, source_target_pairs={{0,8},{4,12},{8,0},{12,4},{16,24},{20,28},{24,16},{28,20},{1,9},{5... | collective-permute-start | bytes 196616 | tf_op jit(solution)/shard_map/ppermute | solution.py:132
  4.5 2.6 %collective-permute-start.4 = (bf16[32,1024]{1,0:T(8,128)(2,1)S(1)}, bf16[32,1024]{1,0:T(8,128)(2,1)S(1)}, u32[]{:S(2)}, u32[]{:S(2)}) collective-permute-start(bf16[32,1024]{1,0:T(8,128)(2,1)S(1)} %slice.27), channel_id=1, source_target_pairs={{0,16},{4,20},{8,24},{12,28},{16,0},{20,4},{24,8},{28,12},{1,17},{... | collective-permute-start | bytes 196616 | tf_op jit(solution)/shard_map/ppermute | solution.py:132
  8.2 3.9 %collective-permute-start.10 = (bf16[32,2048]{1,0:T(8,128)(2,1)S(1)}, bf16[32,2048]{1,0:T(8,128)(2,1)S(1)}, u32[]{:S(2)}, u32[]{:S(2)}) collective-permute-start(bf16[32,2048]{1,0:T(8,128)(2,1)S(1)} %get-tuple-element.66), channel_id=1, source_target_pairs={{0,24},{4,28},{8,16},{12,20},{16,8},{20,12},{24,0},{28,4},{1,25},{... | collective-permute-start | bytes 393224 | tf_op jit(solution)/shard_map/ppermute | solution.py:132
  12.7 6.0 %all-to-all-start = ((bf16[8,8,1024]{2,0,1:T(8,128)(2,1)}), bf16[8,8,1024]{2,0,1:T(8,128)(2,1)S(1)}, u32[]{:S(2)}, u32[]{:S(2)}) async-start(bf16[8,8,1024]{2,0,1:T(8,128)(2,1)} %bitcast.10), calls=%async_computation | async-start | bytes 262144 | tf_op jit(solution)/shard_map/all_to_all | solution.py:210
  24.0 2.4 %collective-permute-start.13 = (bf16[32,2048]{1,0:T(8,128)(2,1)S(1)}, bf16[32,2048]{1,0:T(8,128)(2,1)S(1)}, u32[]{:S(2)}, u32[]{:S(2)}) collective-permute-start(bf16[32,2048]{1,0:T(8,128)(2,1)S(1)} %get-tuple-element.67), channel_id=1, source_target_pairs={{0,16},{4,20},{8,24},{12,28},{16,0},{20,4},{24,8},{28,12},{1,17},{... | collective-permute-start | bytes 393224 | tf_op jit(solution)/shard_map/ppermute | solution.py:132
  31.4 2.7 %collective-permute-start.17 = (bf16[32,2048]{1,0:T(8,128)(2,1)S(1)}, bf16[32,2048]{1,0:T(8,128)(2,1)S(1)}, u32[]{:S(2)}, u32[]{:S(2)}) collective-permute-start(bf16[32,2048]{1,0:T(8,128)(2,1)S(1)} %get-tuple-element.68), channel_id=1, source_target_pairs={{0,16},{4,20},{8,24},{12,28},{16,0},{20,4},{24,8},{28,12},{1,17},{... | collective-permute-start | bytes 393224 | tf_op jit(solution)/shard_map/ppermute | solution.py:132
  34.1 5.1 %collective-permute-done.13.refs_2_ = bf16[32,2048]{1,0:T(8,128)(2,1)S(1)} collective-permute-done((bf16[32,2048]{1,0:T(8,128)(2,1)S(1)}, bf16[32,2048]{1,0:T(8,128)(2,1)S(1)}, u32[]{:S(2)}, u32[]{:S(2)}) %collective-permute-start.13) | collective-permute-done | bytes 131104 | tf_op jit(solution)/shard_map/ppermute | solution.py:132
  39.2 2.9 %collective-permute-start.18 = (bf16[32,2048]{1,0:T(8,128)(2,1)S(1)}, bf16[32,2048]{1,0:T(8,128)(2,1)S(1)}, u32[]{:S(2)}, u32[]{:S(2)}) collective-permute-start(bf16[32,2048]{1,0:T(8,128)(2,1)S(1)} %get-tuple-element.68), channel_id=1, source_target_pairs={{0,24},{4,28},{8,16},{12,20},{16,8},{20,12},{24,0},{28,4},{1,25},{... | collective-permute-start | bytes 393224 | tf_op jit(solution)/shard_map/ppermute | solution.py:132
  45.2 2.5 %collective-permute-done.17.refs_2_ = bf16[32,2048]{1,0:T(8,128)(2,1)S(1)} collective-permute-done((bf16[32,2048]{1,0:T(8,128)(2,1)S(1)}, bf16[32,2048]{1,0:T(8,128)(2,1)S(1)}, u32[]{:S(2)}, u32[]{:S(2)}) %collective-permute-start.17) | collective-permute-done | bytes 131104 | tf_op jit(solution)/shard_map/ppermute | solution.py:132
  50.5 2.4 %collective-permute-done.1 = bf16[64,1024]{0,1:T(8,128)(2,1)S(1)} collective-permute-done((bf16[64,1024]{0,1:T(8,128)(2,1)S(1)}, bf16[64,1024]{0,1:T(8,128)(2,1)S(1)}, u32[]{:S(2)}, u32[]{:S(2)}) %collective-permute-start.1) | collective-permute-done | bytes 131104 | tf_op jit(solution)/shard_map/ppermute | solution.py:132
  54.3 2.5 %collective-permute-done.2 = bf16[64,1024]{0,1:T(8,128)(2,1)S(1)} collective-permute-done((bf16[64,1024]{0,1:T(8,128)(2,1)S(1)}, bf16[64,1024]{0,1:T(8,128)(2,1)S(1)}, u32[]{:S(2)}, u32[]{:S(2)}) %collective-permute-start.2) | collective-permute-done | bytes 131104 | tf_op jit(solution)/shard_map/ppermute | solution.py:132
  60.6 6.3 %one_pass.4 = (f32[3,32,1024]{2,1,0:T(8,128)S(1)}, f32[3,32,1024]{2,1,0:T(8,128)S(1)}, f32[3,8,128]{2,1,0:T(8,128)S(1)}) custom-call(bf16[64,1024]{1,0:T(8,128)(2,1)S(1)} %bitcast.6, bf16[1024,256]{1,0:T(8,128)(2,1)S(1)} %maximum_bitcast_fusion.at_ref, bf16[32,7168]{1,0:T(8,128)(2,1)S(1)} %copy-done, bf16[32,1024]{1,0:T(8,128)(2,1)S(1)} %collective-permute-done.3.refs_1_, ...), custom_call_target="tpu_custom_call" | custom-call | flops 1342177280 | bytes 12582912 | tf_op jit(solution)/shard_map/one_pass/pallas_call | solution.py:95
  67.8 12.5 %one_pass.5 = (f32[3,32,2048]{2,1,0:T(8,128)S(1)}, f32[3,32,2048]{2,1,0:T(8,128)}, f32[3,8,128]{2,1,0:T(8,128)S(1)}) custom-call(bf16[64,1024]{1,0:T(8,128)(2,1)S(1)} %bitcast.7, bf16[1024,256]{1,0:T(8,128)(2,1)S(1)} %maximum_bitcast_fusion.at_ref, bf16[32,7168]{1,0:T(8,128)(2,1)S(1)} %copy-done, bf16[32,2048]{1,0:T(8,128)(2,1)S(1)} %collective-permute-done.8.refs_1_, ...), custom_call_target="tpu_custom_call" | custom-call | flops 2684354560 | bytes 25165824 | tf_op jit(solution)/shard_map/one_pass/pallas_call | solution.py:95
  82.6 11.3 %one_pass.6 = (f32[3,32,2048]{2,1,0:T(8,128)S(1)}, f32[3,32,2048]{2,1,0:T(8,128)S(1)}, f32[3,8,128]{2,1,0:T(8,128)S(1)}) custom-call(bf16[64,1024]{1,0:T(8,128)(2,1)S(1)} %bitcast.8, bf16[1024,256]{1,0:T(8,128)(2,1)S(1)} %maximum_bitcast_fusion.at_ref, bf16[32,7168]{1,0:T(8,128)(2,1)S(1)} %copy-done, bf16[32,2048]{1,0:T(8,128)(2,1)S(1)} %copy-done.8, ...), custom_call_target="tpu_custom_call" | custom-call | flops 2684354560 | bytes 25165824 | tf_op jit(solution)/shard_map/one_pass/pallas_call | solution.py:95
  94.8 11.4 %one_pass.7 = (f32[3,32,2048]{2,1,0:T(8,128)S(1)}, f32[3,32,2048]{2,1,0:T(8,128)S(1)}, f32[3,8,128]{2,1,0:T(8,128)S(1)}) custom-call(bf16[64,1024]{1,0:T(8,128)(2,1)S(1)} %bitcast.9, bf16[1024,256]{1,0:T(8,128)(2,1)S(1)} %maximum_bitcast_fusion.at_ref, bf16[32,7168]{1,0:T(8,128)(2,1)S(1)} %copy-done, bf16[32,2048]{1,0:T(8,128)(2,1)S(1)} %copy-done.12, ...), custom_call_target="tpu_custom_call" | custom-call | flops 2684354560 | bytes 25165824 | tf_op jit(solution)/shard_map/one_pass/pallas_call | solution.py:95
  108.7 5.5 %all-to-all-start.1 = ((f32[32,8,128]{2,1,0:T(8,128)}), f32[32,8,128]{2,1,0:T(8,128)S(1)}, u32[]{:S(2)}, u32[]{:S(2)}) async-start(f32[32,8,128]{2,1,0:T(8,128)} %broadcast_in_dim.2), calls=%async_computation.1 | async-start | bytes 262144 | tf_op jit(solution)/shard_map/all_to_all | solution.py:139
  116.1 6.5 %all-to-all-done.1 = f32[32,8,128]{2,1,0:T(8,128)S(1)} async-done(((f32[32,8,128]{2,1,0:T(8,128)}), f32[32,8,128]{2,1,0:T(8,128)S(1)}, u32[]{:S(2)}, u32[]{:S(2)}) %all-to-all-start.1) | async-done | bytes 131104 | tf_op jit(solution)/shard_map/all_to_all | solution.py:139
  130.9 2.2 %collective-permute-start.22 = (f32[8,1024]{1,0:T(8,128)S(1)}, f32[8,1024]{1,0:T(8,128)S(1)}, u32[]{:S(2)}, u32[]{:S(2)}) collective-permute-start(f32[8,1024]{1,0:T(8,128)S(1)} %get-tuple-element.38), channel_id=1, source_target_pairs={{0,16},{4,20},{8,24},{12,28},{16,0},{20,4},{24,8},{28,12},{1,17},{... | collective-permute-start | bytes 98312 | tf_op jit(solution)/shard_map/ppermute | solution.py:132
  138.5 2.2 %collective-permute-start.34 = (f32[8,2048]{1,0:T(8,128)S(1)}, f32[8,2048]{1,0:T(8,128)S(1)}, u32[]{:S(2)}, u32[]{:S(2)}) collective-permute-start(f32[8,2048]{1,0:T(8,128)S(1)} %get-tuple-element.56), channel_id=1, source_target_pairs={{0,16},{4,20},{8,24},{12,28},{16,0},{20,4},{24,8},{28,12},{1,17},{... | collective-permute-start | bytes 196616 | tf_op jit(solution)/shard_map/ppermute | solution.py:132
  143.1 2.8 %collective-permute-start.23 = (f32[8,1024]{1,0:T(8,128)S(1)}, f32[8,1024]{1,0:T(8,128)S(1)}, u32[]{:S(2)}, u32[]{:S(2)}) collective-permute-start(f32[8,1024]{1,0:T(8,128)S(1)} %get-tuple-element.39), channel_id=1, source_target_pairs={{0,24},{4,28},{8,16},{12,20},{16,8},{20,12},{24,0},{28,4},{1,25},{... | collective-permute-start | bytes 98312 | tf_op jit(solution)/shard_map/ppermute | solution.py:132
  146.7 2.1 %collective-permute-done.23 = f32[8,1024]{1,0:T(8,128)S(1)} collective-permute-done((f32[8,1024]{1,0:T(8,128)S(1)}, f32[8,1024]{1,0:T(8,128)S(1)}, u32[]{:S(2)}, u32[]{:S(2)}) %collective-permute-start.23) | collective-permute-done | bytes 32800 | tf_op jit(solution)/shard_map/ppermute | solution.py:132
  152.4 2.9 %collective-permute-start.26 = (f32[8,2048]{1,0:T(8,128)S(1)}, f32[8,2048]{1,0:T(8,128)S(1)}, u32[]{:S(2)}, u32[]{:S(2)}) collective-permute-start(f32[8,2048]{1,0:T(8,128)S(1)} %get-tuple-element.44), channel_id=1, source_target_pairs={{0,16},{4,20},{8,24},{12,28},{16,0},{20,4},{24,8},{28,12},{1,17},{... | collective-permute-start | bytes 196616 | tf_op jit(solution)/shard_map/ppermute | solution.py:132
  157.4 4.3 %collective-permute-done.26 = f32[8,2048]{1,0:T(8,128)S(1)} collective-permute-done((f32[8,2048]{1,0:T(8,128)S(1)}, f32[8,2048]{1,0:T(8,128)S(1)}, u32[]{:S(2)}, u32[]{:S(2)}) %collective-permute-start.26) | collective-permute-done | bytes 65568 | tf_op jit(solution)/shard_map/ppermute | solution.py:132
  162.7 6.2 %psum.7 = f32[8]{0:T(128)} all-reduce(f32[8]{0:T(128)S(1)} %add_multiply_fusion), channel_id=1, replica_groups=mesh['row'=8,'col'=4] {'col'}, use_global_device_ids=true, to_apply=%region_6.7 | all-reduce | flops 8 | bytes 64 | tf_op jit(solution)/shard_map/psum | solution.py:260
  (132 shorter events, 56.4 us)
Async XLA Ops:
  4.5 15.3 %collective-permute-start.4 = (bf16[32,1024]{1,0:T(8,128)(2,1)S(1)}, bf16[32,1024]{1,0:T(8,128)(2,1)S(1)}, u32[]{:S(2)}, u32[]{:S(2)}) collective-permute-start(bf16[32,1024]{1,0:T(8,128)(2,1)S(1)} %slice.27), channel_id=1, source_target_pairs={{0,16},{4,20},{8,24},{12,28},{16,0},{20,4},{24,8},{28,12},{1,17},{... | collective-permute-start | bytes 196616 | tf_op jit(solution)/shard_map/ppermute | solution.py:132
  7.1 14.8 %collective-permute-start.5 = (bf16[32,1024]{1,0:T(8,128)(2,1)S(1)}, bf16[32,1024]{1,0:T(8,128)(2,1)S(1)}, u32[]{:S(2)}, u32[]{:S(2)}) collective-permute-start(bf16[32,1024]{1,0:T(8,128)(2,1)S(1)} %slice.27), channel_id=1, source_target_pairs={{0,24},{4,28},{8,16},{12,20},{16,8},{20,12},{24,0},{28,4},{1,25},{... | collective-permute-start | bytes 196616 | tf_op jit(solution)/shard_map/ppermute | solution.py:132
  8.2 15.9 %collective-permute-start.10 = (bf16[32,2048]{1,0:T(8,128)(2,1)S(1)}, bf16[32,2048]{1,0:T(8,128)(2,1)S(1)}, u32[]{:S(2)}, u32[]{:S(2)}) collective-permute-start(bf16[32,2048]{1,0:T(8,128)(2,1)S(1)} %get-tuple-element.66), channel_id=1, source_target_pairs={{0,24},{4,28},{8,16},{12,20},{16,8},{20,12},{24,0},{28,4},{1,25},{... | collective-permute-start | bytes 393224 | tf_op jit(solution)/shard_map/ppermute | solution.py:132
  12.1 14.3 %collective-permute-start.8 = (bf16[32,2048]{1,0:T(8,128)(2,1)S(1)}, bf16[32,2048]{1,0:T(8,128)(2,1)S(1)}, u32[]{:S(2)}, u32[]{:S(2)}) collective-permute-start(bf16[32,2048]{1,0:T(8,128)(2,1)S(1)} %get-tuple-element.66), channel_id=1, source_target_pairs={{0,8},{4,12},{8,0},{12,4},{16,24},{20,28},{24,16},{28,20},{1,9},{5... | collective-permute-start | bytes 393224 | tf_op jit(solution)/shard_map/ppermute | solution.py:132
  12.1 16.3 %collective-permute-start.9 = (bf16[32,2048]{1,0:T(8,128)(2,1)S(1)}, bf16[32,2048]{1,0:T(8,128)(2,1)S(1)}, u32[]{:S(2)}, u32[]{:S(2)}) collective-permute-start(bf16[32,2048]{1,0:T(8,128)(2,1)S(1)} %get-tuple-element.66), channel_id=1, source_target_pairs={{0,16},{4,20},{8,24},{12,28},{16,0},{20,4},{24,8},{28,12},{1,17},{... | collective-permute-start | bytes 393224 | tf_op jit(solution)/shard_map/ppermute | solution.py:132
  12.7 46.9 %all-to-all-start = ((bf16[8,8,1024]{2,0,1:T(8,128)(2,1)}), bf16[8,8,1024]{2,0,1:T(8,128)(2,1)S(1)}, u32[]{:S(2)}, u32[]{:S(2)}) async-start(bf16[8,8,1024]{2,0,1:T(8,128)(2,1)} %bitcast.10), calls=%async_computation | async-start | bytes 262144 | tf_op jit(solution)/shard_map/all_to_all | solution.py:210
  19.8 39.8 %collective-permute-start.6 = (bf16[32,7168]{1,0:T(8,128)(2,1)}, bf16[32,7168]{1,0:T(8,128)(2,1)S(1)}, u32[]{:S(2)}, u32[]{:S(2)}) collective-permute-start(bf16[32,7168]{1,0:T(8,128)(2,1)} %refs_0_.7), channel_id=1, source_target_pairs={{0,4},{4,0},{8,12},{12,8},{16,20},{20,16},{24,28},{28,24},{1,5},{5... | collective-permute-start | bytes 1376264 | tf_op jit(solution)/shard_map/ppermute | solution.py:132
  24.0 15.2 %collective-permute-start.13 = (bf16[32,2048]{1,0:T(8,128)(2,1)S(1)}, bf16[32,2048]{1,0:T(8,128)(2,1)S(1)}, u32[]{:S(2)}, u32[]{:S(2)}) collective-permute-start(bf16[32,2048]{1,0:T(8,128)(2,1)S(1)} %get-tuple-element.67), channel_id=1, source_target_pairs={{0,16},{4,20},{8,24},{12,28},{16,0},{20,4},{24,8},{28,12},{1,17},{... | collective-permute-start | bytes 393224 | tf_op jit(solution)/shard_map/ppermute | solution.py:132
  26.4 15.7 %collective-permute-start.14 = (bf16[32,2048]{1,0:T(8,128)(2,1)S(1)}, bf16[32,2048]{1,0:T(8,128)(2,1)S(1)}, u32[]{:S(2)}, u32[]{:S(2)}) collective-permute-start(bf16[32,2048]{1,0:T(8,128)(2,1)S(1)} %get-tuple-element.67), channel_id=1, source_target_pairs={{0,24},{4,28},{8,16},{12,20},{16,8},{20,12},{24,0},{28,4},{1,25},{... | collective-permute-start | bytes 393224 | tf_op jit(solution)/shard_map/ppermute | solution.py:132
  28.3 16.8 %collective-permute-start.16 = (bf16[32,2048]{1,0:T(8,128)(2,1)S(1)}, bf16[32,2048]{1,0:T(8,128)(2,1)S(1)}, u32[]{:S(2)}, u32[]{:S(2)}) collective-permute-start(bf16[32,2048]{1,0:T(8,128)(2,1)S(1)} %get-tuple-element.68), channel_id=1, source_target_pairs={{0,8},{4,12},{8,0},{12,4},{16,24},{20,28},{24,16},{28,20},{1,9},{5... | collective-permute-start | bytes 393224 | tf_op jit(solution)/shard_map/ppermute | solution.py:132
  31.4 16.3 %collective-permute-start.17 = (bf16[32,2048]{1,0:T(8,128)(2,1)S(1)}, bf16[32,2048]{1,0:T(8,128)(2,1)S(1)}, u32[]{:S(2)}, u32[]{:S(2)}) collective-permute-start(bf16[32,2048]{1,0:T(8,128)(2,1)S(1)} %get-tuple-element.68), channel_id=1, source_target_pairs={{0,16},{4,20},{8,24},{12,28},{16,0},{20,4},{24,8},{28,12},{1,17},{... | collective-permute-start | bytes 393224 | tf_op jit(solution)/shard_map/ppermute | solution.py:132
  45.1 11.6 %collective-permute-start.2 = (bf16[64,1024]{0,1:T(8,128)(2,1)S(1)}, bf16[64,1024]{0,1:T(8,128)(2,1)S(1)}, u32[]{:S(2)}, u32[]{:S(2)}) collective-permute-start(bf16[64,1024]{0,1:T(8,128)(2,1)S(1)} %copy.15), channel_id=1, source_target_pairs={{0,3},{1,2},{2,1},{3,0},{4,7},{5,6},{6,5},{7,4},{8,11},{9,10},{10,... | collective-permute-start | bytes 393224 | tf_op jit(solution)/shard_map/ppermute | solution.py:132
  47.7 11.9 %collective-permute-start.7 = (bf16[96,1024]{1,0:T(8,128)(2,1)}, bf16[96,1024]{1,0:T(8,128)(2,1)S(1)}, u32[]{:S(2)}, u32[]{:S(2)}) collective-permute-start(bf16[96,1024]{1,0:T(8,128)(2,1)} %pad_maximum_fusion.3), channel_id=1, source_target_pairs={{0,4},{4,0},{8,12},{12,8},{16,20},{20,16},{24,28},{28,24},{1,5},{5... | collective-permute-start | bytes 589832 | tf_op jit(solution)/shard_map/ppermute | solution.py:132
  49.2 18.6 %collective-permute-start.11 = (bf16[96,2048]{1,0:T(8,128)(2,1)}, bf16[96,2048]{1,0:T(8,128)(2,1)S(1)}, u32[]{:S(2)}, u32[]{:S(2)}) collective-permute-start(bf16[96,2048]{1,0:T(8,128)(2,1)} %pad_maximum_fusion), channel_id=1, source_target_pairs={{0,4},{4,0},{8,12},{12,8},{16,20},{20,16},{24,28},{28,24},{1,5},{5... | collective-permute-start | bytes 1179656 | tf_op jit(solution)/shard_map/ppermute | solution.py:132
  52.8 28.0 %collective-permute-start.15 = (bf16[96,2048]{1,0:T(8,128)(2,1)}, bf16[96,2048]{1,0:T(8,128)(2,1)S(1)}, u32[]{:S(2)}, u32[]{:S(2)}) collective-permute-start(bf16[96,2048]{1,0:T(8,128)(2,1)} %pad_maximum_fusion.1), channel_id=1, source_target_pairs={{0,4},{4,0},{8,12},{12,8},{16,20},{20,16},{24,28},{28,24},{1,5},{5... | collective-permute-start | bytes 1179656 | tf_op jit(solution)/shard_map/ppermute | solution.py:132
  56.8 38.0 %collective-permute-start.19 = (bf16[96,2048]{1,0:T(8,128)(2,1)}, bf16[96,2048]{1,0:T(8,128)(2,1)}, u32[]{:S(2)}, u32[]{:S(2)}) collective-permute-start(bf16[96,2048]{1,0:T(8,128)(2,1)} %pad_maximum_fusion.2), channel_id=1, source_target_pairs={{0,4},{4,0},{8,12},{12,8},{16,20},{20,16},{24,28},{28,24},{1,5},{5... | collective-permute-start | bytes 1179656 | tf_op jit(solution)/shard_map/ppermute | solution.py:132
  80.3 62.8 %collective-permute-start.24 = (f32[3,32,2048]{2,1,0:T(8,128)}, f32[3,32,2048]{2,1,0:T(8,128)S(1)}, u32[]{:S(2)}, u32[]{:S(2)}) collective-permute-start(f32[3,32,2048]{2,1,0:T(8,128)} %get-tuple-element.41), channel_id=1, source_target_pairs={{0,4},{4,0},{8,12},{12,8},{16,20},{20,16},{24,28},{28,24},{1,5},{5... | collective-permute-start | bytes 2359304 | tf_op jit(solution)/shard_map/ppermute | solution.py:132
  108.7 13.8 %all-to-all-start.1 = ((f32[32,8,128]{2,1,0:T(8,128)}), f32[32,8,128]{2,1,0:T(8,128)S(1)}, u32[]{:S(2)}, u32[]{:S(2)}) async-start(f32[32,8,128]{2,1,0:T(8,128)} %broadcast_in_dim.2), calls=%async_computation.1 | async-start | bytes 262144 | tf_op jit(solution)/shard_map/all_to_all | solution.py:139
  114.2 14.3 %collective-permute-start.20 = (f32[3,32,1024]{2,1,0:T(8,128)}, f32[3,32,1024]{2,1,0:T(8,128)S(1)}, u32[]{:S(2)}, u32[]{:S(2)}) collective-permute-start(f32[3,32,1024]{2,1,0:T(8,128)} %copy-done.23), channel_id=1, source_target_pairs={{0,4},{4,0},{8,12},{12,8},{16,20},{20,16},{24,28},{28,24},{1,5},{5... | collective-permute-start | bytes 1179656 | tf_op jit(solution)/shard_map/ppermute | solution.py:132
  127.1 11.4 %collective-permute-start.28 = (f32[32,2048]{1,0:T(8,128)S(1)}, f32[32,2048]{1,0:T(8,128)S(1)}, u32[]{:S(2)}, u32[]{:S(2)}) collective-permute-start(f32[32,2048]{1,0:T(8,128)S(1)} %blended.8), channel_id=1, source_target_pairs={{0,4},{4,0},{8,12},{12,8},{16,20},{20,16},{24,28},{28,24},{1,5},{5... | collective-permute-start | bytes 786440 | tf_op jit(solution)/shard_map/ppermute | solution.py:132
  130.9 12.2 %collective-permute-start.22 = (f32[8,1024]{1,0:T(8,128)S(1)}, f32[8,1024]{1,0:T(8,128)S(1)}, u32[]{:S(2)}, u32[]{:S(2)}) collective-permute-start(f32[8,1024]{1,0:T(8,128)S(1)} %get-tuple-element.38), channel_id=1, source_target_pairs={{0,16},{4,20},{8,24},{12,28},{16,0},{20,4},{24,8},{28,12},{1,17},{... | collective-permute-start | bytes 98312 | tf_op jit(solution)/shard_map/ppermute | solution.py:132
  135.6 15.3 %collective-permute-start.33 = (f32[8,2048]{1,0:T(8,128)S(1)}, f32[8,2048]{1,0:T(8,128)S(1)}, u32[]{:S(2)}, u32[]{:S(2)}) collective-permute-start(f32[8,2048]{1,0:T(8,128)S(1)} %get-tuple-element.55), channel_id=1, source_target_pairs={{0,8},{4,12},{8,0},{12,4},{16,24},{20,28},{24,16},{28,20},{1,9},{5... | collective-permute-start | bytes 196616 | tf_op jit(solution)/shard_map/ppermute | solution.py:132
  138.5 13.3 %collective-permute-start.34 = (f32[8,2048]{1,0:T(8,128)S(1)}, f32[8,2048]{1,0:T(8,128)S(1)}, u32[]{:S(2)}, u32[]{:S(2)}) collective-permute-start(f32[8,2048]{1,0:T(8,128)S(1)} %get-tuple-element.56), channel_id=1, source_target_pairs={{0,16},{4,20},{8,24},{12,28},{16,0},{20,4},{24,8},{28,12},{1,17},{... | collective-permute-start | bytes 196616 | tf_op jit(solution)/shard_map/ppermute | solution.py:132
  143.1 12.2 %collective-permute-start.29 = (f32[8,2048]{1,0:T(8,128)S(1)}, f32[8,2048]{1,0:T(8,128)S(1)}, u32[]{:S(2)}, u32[]{:S(2)}) collective-permute-start(f32[8,2048]{1,0:T(8,128)S(1)} %get-tuple-element.49), channel_id=1, source_target_pairs={{0,8},{4,12},{8,0},{12,4},{16,24},{20,28},{24,16},{28,20},{1,9},{5... | collective-permute-start | bytes 196616 | tf_op jit(solution)/shard_map/ppermute | solution.py:132
  (40 other events, 487.3 us)
